TPU v7x, 32 devices: a whole 2x2x4 slice. The times are simulated.
32 devices in a mesh: groups: 2 (over y), emit: 4 (over z), recv: 4 (over x, core).
Axes of the slice: x: 2, y: 2, z: 4, core: 2. Of those that a mesh axis runs over, the one named last changes fastest.
Arguments:
- positions: float32 [3, 8192], P(None, ('groups', 'emit', 'recv')), parts along dimension 1, may hold values from 0 to 1
- angles: float32 [2, 8192], P(None, ('groups', 'emit', 'recv')), parts along dimension 1, may hold values from -3.140625 to 3.140625
- areas: float32 [8192], P(('groups', 'emit', 'recv')), parts along dimension 0, may hold values from 0.00024414062 to 0.00390625
- emissivity: float32 [8192], P(('groups', 'emit', 'recv')), parts along dimension 0, may hold values from 0.1 to 0.9
- emission: float32 [32, 8192], P(None, ('groups', 'emit', 'recv')), parts along dimension 1, may hold values from 0.5 to 2
- radiosity_in: float32 [32, 8192], P(None, ('groups', 'emit', 'recv')), parts along dimension 1, may hold values from 0.2 to 2
- adjoint_in: float32 [32, 8192], P(None, ('groups', 'emit', 'recv')), parts along dimension 1, may hold values from 0 to 1.5
- visibility: int32 [64, 32], P(('groups', 'emit')), parts along dimension 0, may hold values 0 or 1
- inlet_patches: int32 [4096], P('groups'), parts along dimension 0, may hold values from 0 to 4095
- inlet_weights: float32 [32, 4096], P(None, 'groups'), parts along dimension 1, may hold values from 0.5 to 2
Outputs:
- radiosity_out: float32 [32, 8192], P(None, ('groups', 'emit', 'recv')), parts along dimension 1
- adjoint_out: float32 [32, 8192], P(None, ('groups', 'emit', 'recv')), parts along dimension 1
- emissivity_grad: float32 [8192], P(('groups', 'emit', 'recv')), parts along dimension 0
There are 2 independent parts, one for each index of `groups`. A program takes and returns all parts, laid end to end along the dimension named above; each array names one. Nothing has to cross between parts.
Inputs may be any that keep to these rules, and one draw needn't show every extreme that they name: `inlet_patches`: an inlet patch may be listed more than once.
All inputs are finite; a program needn't handle non-finite values. No bound on the sum of `visibility` on one device may be relied on, other than what follows from the above.
Results may differ from a plain program's by a relative error of at most 0.0003.
Values may be sent and summed in bfloat16 or wider, within the bound.
No kernel may reach another device: no remote copies, remote signals or barrier semaphores. Data moves between devices by JAX's collectives and lax.ppermute only.
A program may use at most 64 MiB of HBM per device.

v0:
```python
import math
import jax
import jax.numpy as jnp
from jax import lax
from jax.sharding import PartitionSpec as P

BLK = 128


def patch_geometry(positions, angles, areas):
    polar = angles[0]
    azimuth = angles[1]
    normal = jnp.stack(
        [jnp.sin(polar) * jnp.cos(azimuth), jnp.sin(polar) * jnp.sin(azimuth), jnp.cos(polar)]
    )
    return jnp.concatenate([positions, normal, areas[None, :]], axis=0)


def view_tile(row_geom, col_geom, block_mask):
    delta_x = col_geom[0][None, :] - row_geom[0][:, None]
    delta_y = col_geom[1][None, :] - row_geom[1][:, None]
    delta_z = col_geom[2][None, :] - row_geom[2][:, None]
    dist_sq = delta_x * delta_x + delta_y * delta_y + delta_z * delta_z
    cos_emit = jnp.maximum(
        row_geom[3][:, None] * delta_x
        + row_geom[4][:, None] * delta_y
        + row_geom[5][:, None] * delta_z,
        0.0,
    )
    cos_recv = jnp.maximum(
        -(
            col_geom[3][None, :] * delta_x
            + col_geom[4][None, :] * delta_y
            + col_geom[5][None, :] * delta_z
        ),
        0.0,
    )
    patch_area = row_geom[6][:, None]
    spread = dist_sq + patch_area
    kernel = cos_emit * cos_recv * patch_area / (math.pi * spread * spread)
    row_blocks, col_blocks = block_mask.shape
    rows_total = row_geom.shape[1]
    cols_total = col_geom.shape[1]
    expanded = jnp.broadcast_to(
        block_mask[:, None, :, None],
        (row_blocks, rows_total // row_blocks, col_blocks, cols_total // col_blocks),
    ).reshape(rows_total, cols_total)
    return (expanded * kernel).astype(jnp.bfloat16)


def block_width():
    return 128


def local(
    positions,
    angles,
    areas,
    emissivity,
    emission,
    radiosity_in,
    adjoint_in,
    visibility,
    inlet_patches,
    inlet_weights,
):
    emit_count = lax.axis_size("emit")
    recv_count = lax.axis_size("recv")
    emit_index = lax.axis_index("emit")
    recv_index = lax.axis_index("recv")
    own_count = areas.shape[0]
    cases = emission.shape[0]
    geometry = patch_geometry(positions, angles, areas)
    reflect = 1.0 - emissivity
    own_weights = (reflect[None, :] * adjoint_in).astype(jnp.bfloat16)
    own_values = radiosity_in.astype(jnp.bfloat16)
    mask_rows = visibility.shape[0]
    per_block = visibility.shape[1] // emit_count
    own_blocks = own_count // BLK
    folded_mask = visibility.astype(jnp.float32).reshape(mask_rows, emit_count, per_block)
    tile_mask = lax.dynamic_slice_in_dim(
        folded_mask, recv_index * own_blocks, own_blocks, 2
    ).reshape(mask_rows, emit_count * own_blocks)
    row_total = own_count * recv_count
    col_total = own_count * emit_count
    row_values = lax.all_gather(own_values, "recv", axis=1, tiled=True)
    col_weight = lax.all_gather(own_weights, "emit", axis=1, tiled=True)
    start_state = (
        jnp.zeros((cases, col_total), jnp.float32),
        jnp.zeros((cases, row_total), jnp.float32),
    )
    col_geom = lax.all_gather(geometry, "emit", axis=1, tiled=True)
    geom_piece = lax.all_gather(geometry, "recv", axis=1, tiled=True)
    count = geom_piece.shape[1]
    width = block_width()

    def inner(number, state):
        fwd_total, adj_total = state
        offset = number * width
        geom_part = lax.dynamic_slice_in_dim(geom_piece, offset, width, 1)
        value_part = lax.dynamic_slice_in_dim(row_values, offset, width, 1)
        mask_part = lax.dynamic_slice_in_dim(tile_mask, offset // BLK, width // BLK, 0)
        tile = view_tile(geom_part, col_geom, mask_part)
        fwd_total = fwd_total + jnp.dot(value_part, tile, preferred_element_type=jnp.float32)
        adj_part = lax.dot_general(
            col_weight, tile, (((1,), (1,)), ((), ())), preferred_element_type=jnp.float32
        )
        adj_total = lax.dynamic_update_slice_in_dim(adj_total, adj_part, offset, 1)
        return (fwd_total, adj_total)

    forward, adjoint = lax.fori_loop(0, count // width, inner, start_state)
    incoming = lax.psum_scatter(forward, "emit", scatter_dimension=1, tiled=True)
    returned = lax.psum_scatter(adjoint, "recv", scatter_dimension=1, tiled=True)
    own_ids = (emit_index * recv_count + recv_index) * own_count + lax.iota(jnp.int32, own_count)
    selector = (inlet_patches[:, None] == own_ids[None, :]).astype(jnp.float32)
    source = jnp.dot(
        inlet_weights, selector, precision=lax.Precision.HIGHEST, preferred_element_type=jnp.float32
    )
    radiosity_out = emissivity[None, :] * emission + reflect[None, :] * incoming
    adjoint_out = source + returned
    emissivity_grad = jnp.sum(adjoint_out * (emission - incoming), axis=0)
    return (radiosity_out, adjoint_out, emissivity_grad)


def solution(mesh):
    placed = (
        P(None, ("groups", "emit", "recv")),
        P(None, ("groups", "emit", "recv")),
        P(("groups", "emit", "recv")),
        P(("groups", "emit", "recv")),
        P(None, ("groups", "emit", "recv")),
        P(None, ("groups", "emit", "recv")),
        P(None, ("groups", "emit", "recv")),
        P(("groups", "emit"), None),
        P("groups"),
        P(None, "groups"),
    )
    return jax.shard_map(
        local,
        mesh=mesh,
        in_specs=placed,
        out_specs=(
            P(None, ("groups", "emit", "recv")),
            P(None, ("groups", "emit", "recv")),
            P(("groups", "emit", "recv")),
        ),
        check_vma=False,
    )
```

profile of v0, /device:TPU:0, one launch (start us, length us, event | category | flops | bytes accessed | tf_op | source)
XLA Modules:
  0.0 115.8 jit_solution(4974398801967030085)
XLA Ops:
  7.2 0.8 slice_cosine_fusion
  8.1 0.7 concatenate.3
  8.8 14.8 %all_gather.14 = f32[7,1024]{1,0:T(8,128)S(1)} all-gather(f32[7,256]{1,0:T(8,128)S(1)} %concatenate.3), channel_id=1, replica_groups=mesh['groups'=2,'emit'=4,'recv'=4] {'emit'}, dimensions={1}, use_global_device_ids=true | all-gather | bytes 35840 | tf_op jit(solution)/shard_map/all_gather | solution.py:92
  23.6 5.2 %all_gather.13 = f32[7,1024]{1,0:T(8,128)S(1)} all-gather(f32[7,256]{1,0:T(8,128)S(1)} %concatenate.3), channel_id=1, replica_groups=mesh['groups'=2,'emit'=4,'recv'=4] {'recv'}, dimensions={1}, use_global_device_ids=true | all-gather | bytes 35840 | tf_op jit(solution)/shard_map/all_gather | solution.py:93
  28.8 0.7 broadcast_subtract_fusion
  29.5 0.7 convert_element_type.21
  30.1 0.1 copy.15
  30.3 0.8 convert_element_type.20
  31.1 5.2 %all_gather.12 = bf16[32,1024]{1,0:T(8,128)(2,1)S(1)} all-gather(bf16[32,256]{1,0:T(8,128)(2,1)S(1)} %convert_element_type.20), channel_id=1, replica_groups=mesh['groups'=2,'emit'=4,'recv'=4] {'recv'}, dimensions={1}, use_global_device_ids=true | all-gather | bytes 81920 | tf_op jit(solution)/shard_map/all_gather | solution.py:86
  36.3 13.1 %all_gather.15 = bf16[32,1024]{1,0:T(8,128)(2,1)S(1)} all-gather(bf16[32,256]{1,0:T(8,128)(2,1)S(1)} %multiply_convert_fusion), channel_id=1, replica_groups=mesh['groups'=2,'emit'=4,'recv'=4] {'emit'}, dimensions={1}, use_global_device_ids=true | all-gather | bytes 81920 | tf_op jit(solution)/shard_map/all_gather | solution.py:87
  49.4 13.7 %while.18 = (s32[]{:T(128)}, f32[32,1024]{1,0:T(8,128)S(1)}, f32[32,1024]{1,0:T(8,128)S(1)}, bf16[32,1024]{1,0:T(8,128)(2,1)S(1)}, f32[8,8]{1,0:T(8,128)S(1)}, /...) while((s32[]{:T(128)}, f32[32,1024]{1,0:T(8,128)S(1)}, ...), condition=%wide.region_1.2_spmd.clone, body=%wide.region_0.1_spmd.clone.sunk | while | flops 24444952 | bytes 484852 | solution.py:111
  49.6 0.8 convolution_add_fusion.2
  50.4 0.8 fusion.47
  51.3 0.8 convolution_add_fusion.2
  52.1 0.8 fusion.47
  53.0 0.8 convolution_add_fusion.2
  53.8 0.8 fusion.47
  54.7 0.8 convolution_add_fusion.2
  55.5 0.8 fusion.47
  56.4 0.8 convolution_add_fusion.2
  57.2 0.8 fusion.47
  58.1 0.8 convolution_add_fusion.2
  58.9 0.8 fusion.47
  59.8 0.8 convolution_add_fusion.2
  60.6 0.8 fusion.47
  61.5 0.8 convolution_add_fusion.2
  62.4 0.8 fusion.47
  63.2 0.6 copy-done.1
  63.9 0.7 reduce-scatter.3.cloned.1.call-update
  64.6 20.0 %reduce-scatter.5.cloned.1.call-done = f32[32,256]{1,0:T(8,128)} async-done(((f32[32,1024]{1,0:T(8,128)}), f32[32,256]{1,0:T(8,128)}) %reduce-scatter.5.cloned.1.call-update) | async-done | bytes 32784 | tf_op jit(solution)/shard_map/reduce_scatter | solution.py:113
  84.6 21.6 %reduce-scatter.3.cloned.1.call-done = f32[32,256]{1,0:T(8,128)} async-done(((f32[32,1024]{1,0:T(8,128)}), f32[32,256]{1,0:T(8,128)}) %reduce-scatter.3.cloned.1.call-update) | async-done | bytes 32784 | tf_op jit(solution)/shard_map/reduce_scatter | solution.py:112
  106.2 2.8 %multiply_reduce_fusion = (f32[256]{0:T(256)}, f32[32,256]{1,0:T(8,128)}, f32[32,256]{1,0:T(8,128)}) fusion(f32[32,256]{1,0:T(8,128)S(1)} %copy-done.5, f32[32,256]{1,0:T(8,128)} %reduce-scatter.3.cloned.1.call-done, f32[256]{0:T(256)S(1)} %broadcast_subtract_fusion, f32[256]{0:T(256)S(1)} %copy-done.4, f32[32,256]{1,0:T(8,128)} %reduce-scatter.5.cloned.1.call-done, ...), kind=kOutput, calls=%fused_computation.47 | convolution fusion | flops 201907968 | bytes 438272 | tf_op jit(solution)/shard_map/dot_general | solution.py:116
  (62 shorter events, 1.1 us)
Async XLA Ops:
  7.2 99.0 %copy-start = (f32[32,2048]{1,0:T(8,128)S(1)}, f32[32,2048]{1,0:T(8,128)}, u32[]{:S(2)}) copy-start(f32[32,2048]{1,0:T(8,128)} %param.21) | copy-start | bytes 786436
  7.2 29.1 %copy-start.3 = (f32[32,256]{1,0:T(8,128)S(1)}, f32[32,256]{1,0:T(8,128)}, u32[]{:S(2)}) copy-start(f32[32,256]{1,0:T(8,128)} %param.18) | copy-start | bytes 98308
  7.2 77.4 %reduce-scatter.5.cloned.1.call-start = ((), (), s32[]{:S(2)}) async-start(), calls=%async_computation.3 | async-start | bytes 163840 | tf_op jit(solution)/shard_map/reduce_scatter | solution.py:113
  63.1 0.7 copy-start.1
  63.1 0.7 copy-start.2
  63.1 43.0 %copy-start.4 = (f32[256]{0:T(256)S(1)}, f32[256]{0:T(256)}, u32[]{:S(2)}) copy-start(f32[256]{0:T(256)} %param.15) | copy-start | bytes 3076
  63.2 43.0 %copy-start.5 = (f32[32,256]{1,0:T(8,128)S(1)}, f32[32,256]{1,0:T(8,128)}, u32[]{:S(2)}) copy-start(f32[32,256]{1,0:T(8,128)} %param.16) | copy-start | bytes 98308
  63.2 43.0 %copy-start.6 = (s32[2048]{0:T(1024)S(1)}, s32[2048]{0:T(1024)}, u32[]{:S(2)}) copy-start(s32[2048]{0:T(1024)} %param.20) | copy-start | bytes 24580
  63.8 42.3 %reduce-scatter.3.cloned.1.call-start = ((), (), s32[]{:S(2)}) async-start(), calls=%async_computation.2 | async-start | bytes 163840 | tf_op jit(solution)/shard_map/reduce_scatter | solution.py:112
Sparse Core Ops, SparseCore 0:
  63.9 20.5 reduce-scatter.4
  86.9 19.1 reduce-scatter.2
where the time goes:
time: 116 us
  waiting for transfers between devices  42.3 us (36%)
  blocking collectives  38.3 us (33%)
  matrix products  15.3 us (13%)
  between operations  14.1 us (12%)
  other arithmetic  2.97 us (3%)
  local copies, waits for them, and re-layouts  2.42 us (2%)
    reduce_scatter x1, waiting for transfers between devices, local(): lax.psum_scatter(forward, 'emit', scatter_dimension=1, tiled=True)  21.6 us
    reduce_scatter x1, waiting for transfers between devices, local(): lax.psum_scatter(adjoint, 'recv', scatter_dimension=1, tiled=True)  20 us
    all_gather x1, blocking collectives, local(): col_geom = lax.all_gather(geometry, 'emit', axis=1, tiled=True)  14.8 us
    all_gather x1, blocking collectives, local(): col_weight = lax.all_gather(own_weights, 'emit', axis=1, tiled=True)  13.1 us
    dot_general x8, matrix products, inner(): jnp.dot(value_part, tile, preferred_element_type=jnp.float32)  6.43 us
    dot_general x8, matrix products, inner(): lax.dot_general(col_weight, tile, (((1,), (1,)), ((), ())), preferred_ele...  6.15 us
    all_gather x1, blocking collectives, local(): row_values = lax.all_gather(own_values, 'recv', axis=1, tiled=True)  5.23 us
    all_gather x1, blocking collectives, local(): geom_piece = lax.all_gather(geometry, 'recv', axis=1, tiled=True)  5.18 us
  transfers between devices with their start and end apart: 2, of which 2 were waited for; matrix products, arithmetic and copies ran while one was open for 0% of the time, Pallas kernels for 0%

commit v1 on v0

--- a/solution.py
+++ b/solution.py
@@ -83,7 +83,15 @@
     ).reshape(mask_rows, emit_count * own_blocks)
     row_total = own_count * recv_count
     col_total = own_count * emit_count
-    row_values = lax.all_gather(own_values, "recv", axis=1, tiled=True)
+    ways, here = (lax.axis_size("recv"), lax.axis_index("recv"))
+    grown, reach = (own_values, 1)
+    while reach < ways:
+        theirs = lax.ppermute(grown, "recv", [(d, d ^ reach) for d in range(ways)])
+        mine_first = jnp.concatenate([grown, theirs], axis=1)
+        theirs_first = jnp.concatenate([theirs, grown], axis=1)
+        grown = jnp.where(here & reach == 0, mine_first, theirs_first)
+        reach = 2 * reach
+    row_values = grown
     col_weight = lax.all_gather(own_weights, "emit", axis=1, tiled=True)
     start_state = (
         jnp.zeros((cases, col_total), jnp.float32),

time: 116 us -> 112 us (0.966)
  blocking collectives: 38.3 us -> 32.6 us
  other arithmetic: 2.97 us -> 5.73 us
  waiting for transfers between devices: 42.3 us -> 39.7 us
  starting transfers between devices: 0.08 us -> 2.09 us
  matrix products: 15.3 us -> 14.1 us
    all_gather x1 -> x0, blocking collectives: 5.23 us -> none  [local(): row_values = lax.all_gather(own_values, 'recv', axis=1, tiled=True)]
    ppermute x0 -> x2, starting transfers between devices: none -> 2.01 us  [local(): theirs = lax.ppermute(grown, 'recv', [(d, d ^ reach) for d in range(ways)])]
    reduce_sum x0 -> x1, other arithmetic: none -> 1.95 us  [local(): emissivity_grad = jnp.sum(adjoint_out * (emission - incoming), axis=0)]
    reduce_scatter x1, waiting for transfers between devices: 21.6 us -> 20 us  [local(): lax.psum_scatter(forward, 'emit', scatter_dimension=1, tiled=True)]
    dot_general x1, matrix products: 2.76 us -> 1.56 us  [local(): jnp.dot(inlet_weights, selector, precision=lax.Precision.HIGHEST, preferr...]
  transfers between devices with their start and end apart: 2 -> 4, of which waited for: 2 -> 2; matrix products, arithmetic and copies ran while one was open for 0% -> 5% of each run, Pallas kernels for 0% -> 0%
where the time goes in v1:
time: 112 us; the launch traced here: 111 us
  waiting for transfers between devices  39.7 us (35%)
  blocking collectives  32.6 us (29%)
  between operations  14.2 us (13%)
  matrix products  14.1 us (13%)
  other arithmetic  5.73 us (5%)
  local copies, waits for them, and re-layouts  2.43 us (2%)
  starting transfers between devices  2.09 us (2%)
    reduce_scatter x1, waiting for transfers between devices, local(): lax.psum_scatter(forward, 'emit', scatter_dimension=1, tiled=True)  20 us
    reduce_scatter x1, waiting for transfers between devices, local(): lax.psum_scatter(adjoint, 'recv', scatter_dimension=1, tiled=True)  19 us
    all_gather x1, blocking collectives, local(): col_geom = lax.all_gather(geometry, 'emit', axis=1, tiled=True)  14.4 us
    all_gather x1, blocking collectives, local(): col_weight = lax.all_gather(own_weights, 'emit', axis=1, tiled=True)  13.1 us
    dot_general x8, matrix products, inner(): jnp.dot(value_part, tile, preferred_element_type=jnp.float32)  6.43 us
    dot_general x8, matrix products, inner(): lax.dot_general(col_weight, tile, (((1,), (1,)), ((), ())), preferred_ele...  6.15 us
    all_gather x1, blocking collectives, local(): geom_piece = lax.all_gather(geometry, 'recv', axis=1, tiled=True)  5.18 us
  transfers between devices with their start and end apart: 4, of which 2 were waited for; matrix products, arithmetic and copies ran while one was open for 5% of the time, Pallas kernels for 0%

profile of v1, /device:TPU:0, one launch (start us, length us, event | category | flops | bytes accessed | tf_op | source)
XLA Modules:
  0.0 111.2 jit_solution(1433424895633718646)
XLA Ops:
  7.2 0.8 convert_element_type.20
  8.5 0.7 broadcast_subtract_fusion
  9.2 0.8 slice_cosine_fusion
  10.0 0.7 convert_element_type.21
  10.8 0.8 multiply_convert_fusion
  11.6 0.7 concatenate.19
  12.3 14.4 %all_gather.10 = f32[7,1024]{1,0:T(8,128)S(1)} all-gather(f32[7,256]{1,0:T(8,128)S(1)} %concatenate.19), channel_id=1, replica_groups=mesh['groups'=2,'emit'=4,'recv'=4] {'emit'}, dimensions={1}, use_global_device_ids=true | all-gather | bytes 35840 | tf_op jit(solution)/shard_map/all_gather | solution.py:100
  26.7 1.6 %collective-permute-start.1 = (bf16[32,512]{1,0:T(8,128)(2,1)S(1)}, bf16[32,512]{1,0:T(8,128)(2,1)S(1)}, u32[]{:S(2)}, u32[]{:S(2)}) collective-permute-start(bf16[32,512]{1,0:T(8,128)(2,1)S(1)} %maximum_select_fusion.1), channel_id=1, source_target_pairs={{0,2},{1,3},{2,0},{3,1},{4,6},{5,7},{6,4},{7,5},{8,10},{9,11},{10,... | collective-permute-start | bytes 98312 | tf_op jit(solution)/shard_map/ppermute | solution.py:89
  28.3 5.2 %all_gather.9 = f32[7,1024]{1,0:T(8,128)S(1)} all-gather(f32[7,256]{1,0:T(8,128)S(1)} %concatenate.19), channel_id=1, replica_groups=mesh['groups'=2,'emit'=4,'recv'=4] {'recv'}, dimensions={1}, use_global_device_ids=true | all-gather | bytes 35840 | tf_op jit(solution)/shard_map/all_gather | solution.py:101
  33.4 13.1 %all_gather.11 = bf16[32,1024]{1,0:T(8,128)(2,1)S(1)} all-gather(bf16[32,256]{1,0:T(8,128)(2,1)S(1)} %multiply_convert_fusion), channel_id=1, replica_groups=mesh['groups'=2,'emit'=4,'recv'=4] {'emit'}, dimensions={1}, use_global_device_ids=true | all-gather | bytes 81920 | tf_op jit(solution)/shard_map/all_gather | solution.py:95
  46.6 13.7 %while.18 = (s32[]{:T(128)}, f32[32,1024]{1,0:T(8,128)S(1)}, f32[32,1024]{1,0:T(8,128)S(1)}, bf16[32,1024]{1,0:T(8,128)(2,1)S(1)}, f32[8,8]{1,0:T(8,128)S(1)}, /...) while((s32[]{:T(128)}, f32[32,1024]{1,0:T(8,128)S(1)}, ...), condition=%wide.region_1.2_spmd.clone, body=%wide.region_0.1_spmd.clone.sunk | while | flops 24444952 | bytes 484852 | solution.py:119
  46.8 0.8 convolution_add_fusion.2
  47.6 0.8 fusion.47
  48.5 0.8 convolution_add_fusion.2
  49.3 0.8 fusion.47
  50.2 0.8 convolution_add_fusion.2
  51.0 0.8 fusion.47
  51.9 0.8 convolution_add_fusion.2
  52.7 0.8 fusion.47
  53.6 0.8 convolution_add_fusion.2
  54.4 0.8 fusion.47
  55.3 0.8 convolution_add_fusion.2
  56.1 0.8 fusion.47
  57.0 0.8 convolution_add_fusion.2
  57.8 0.8 fusion.47
  58.7 0.8 convolution_add_fusion.2
  59.5 0.8 fusion.47
  61.0 0.7 reduce-scatter.3.cloned.1.call-update
  61.8 19.0 %reduce-scatter.5.cloned.1.call-done = f32[32,256]{1,0:T(8,128)} async-done(((f32[32,1024]{1,0:T(8,128)}), f32[32,256]{1,0:T(8,128)}) %reduce-scatter.5.cloned.1.call-update) | async-done | bytes 32784 | tf_op jit(solution)/shard_map/reduce_scatter | solution.py:121
  80.8 1.6 %fusion.26 = f32[32,256]{1,0:T(8,128)S(1)} fusion(f32[32,256]{1,0:T(8,128)} %reduce-scatter.5.cloned.1.call-done, f32[32,2048]{1,0:T(8,128)S(1)} %copy-done, s32[256]{0:T(256)S(1)} %iota_add_fusion, s32[2048]{0:T(1024)S(1)} %copy-done.6), kind=kOutput, calls=%fused_computation.44 | convolution fusion | flops 201859072 | bytes 336896 | tf_op jit(solution)/shard_map/dot_general | solution.py:124
  82.4 20.0 %reduce-scatter.3.cloned.1.call-done = f32[32,256]{1,0:T(8,128)} async-done(((f32[32,1024]{1,0:T(8,128)}), f32[32,256]{1,0:T(8,128)}) %reduce-scatter.3.cloned.1.call-update) | async-done | bytes 32784 | tf_op jit(solution)/shard_map/reduce_scatter | solution.py:120
  102.4 1.9 %multiply_reduce_fusion = (f32[256]{0:T(256)}, f32[32,256]{1,0:T(8,128)}) fusion(f32[32,256]{1,0:T(8,128)S(1)} %fusion.26, f32[32,256]{1,0:T(8,128)S(1)} %copy-done.3, f32[32,256]{1,0:T(8,128)} %reduce-scatter.3.cloned.1.call-done, f32[256]{0:T(256)S(1)} %broadcast_subtract_fusion, f32[256]{0:T(256)S(1)} %copy-done.5), kind=kLoop, calls=%fused_computation.49 | loop fusion | flops 48896 | bytes 134144 | tf_op jit(solution)/shard_map/reduce_sum | solution.py:129
  (68 shorter events, 2.3 us)
Async XLA Ops:
  7.2 73.6 %copy-start = (f32[32,2048]{1,0:T(8,128)S(1)}, f32[32,2048]{1,0:T(8,128)}, u32[]{:S(2)}) copy-start(f32[32,2048]{1,0:T(8,128)} %param.21) | copy-start | bytes 786436
  7.2 73.6 %reduce-scatter.5.cloned.1.call-start = ((), (), s32[]{:S(2)}) async-start(), calls=%async_computation.3 | async-start | bytes 163840 | tf_op jit(solution)/shard_map/reduce_scatter | solution.py:121
  8.0 18.7 %collective-permute-start = (bf16[32,256]{1,0:T(8,128)(2,1)S(1)}, bf16[32,256]{1,0:T(8,128)(2,1)S(1)}, u32[]{:S(2)}, u32[]{:S(2)}) collective-permute-start(bf16[32,256]{1,0:T(8,128)(2,1)S(1)} %convert_element_type.20), channel_id=1, source_target_pairs={{0,1},{1,0},{2,3},{3,2},{4,5},{5,4},{6,7},{7,6},{8,9},{9,8},{10,11... | collective-permute-start | bytes 49160 | tf_op jit(solution)/shard_map/ppermute | solution.py:89
  26.7 19.9 %collective-permute-start.1 = (bf16[32,512]{1,0:T(8,128)(2,1)S(1)}, bf16[32,512]{1,0:T(8,128)(2,1)S(1)}, u32[]{:S(2)}, u32[]{:S(2)}) collective-permute-start(bf16[32,512]{1,0:T(8,128)(2,1)S(1)} %maximum_select_fusion.1), channel_id=1, source_target_pairs={{0,2},{1,3},{2,0},{3,1},{4,6},{5,7},{6,4},{7,5},{8,10},{9,11},{10,... | collective-permute-start | bytes 98312 | tf_op jit(solution)/shard_map/ppermute | solution.py:89
  60.3 0.7 copy-start.1
  60.3 0.7 copy-start.2
  60.3 20.5 %copy-start.6 = (s32[2048]{0:T(1024)S(1)}, s32[2048]{0:T(1024)}, u32[]{:S(2)}) copy-start(s32[2048]{0:T(1024)} %param.20) | copy-start | bytes 24580
  61.0 41.4 %reduce-scatter.3.cloned.1.call-start = ((), (), s32[]{:S(2)}) async-start(), calls=%async_computation.2 | async-start | bytes 163840 | tf_op jit(solution)/shard_map/reduce_scatter | solution.py:120
  61.7 40.6 %copy-start.3 = (f32[32,256]{1,0:T(8,128)S(1)}, f32[32,256]{1,0:T(8,128)}, u32[]{:S(2)}) copy-start(f32[32,256]{1,0:T(8,128)} %param.16) | copy-start | bytes 98308
  61.7 40.6 %copy-start.5 = (f32[256]{0:T(256)S(1)}, f32[256]{0:T(256)}, u32[]{:S(2)}) copy-start(f32[256]{0:T(256)} %param.15) | copy-start | bytes 3076
  82.4 21.9 %copy-start.4 = (f32[32,256]{1,0:T(8,128)}, f32[32,256]{1,0:T(8,128)S(1)}, u32[]{:S(2)}) copy-start(f32[32,256]{1,0:T(8,128)S(1)} %fusion.26) | copy-start | bytes 98308
Sparse Core Ops, SparseCore 0:
  61.1 19.6 reduce-scatter.4
  83.1 19.1 reduce-scatter.2
